TPU v7x, 512 devices: a whole 4x8x8 slice. The times are simulated.
512 devices in a mesh: ctx: 64 (over z, y), head: 8 (over x, core).
Axes of the slice: x: 4, y: 8, z: 8, core: 2. Of those that a mesh axis runs over, the one named last changes fastest.
Arguments:
- queries: bfloat16 [49152, 3072], P(('ctx', 'head')), may hold values from -20 to 20
- keys: bfloat16 [49152, 3072], P(('ctx', 'head')), may hold values from -6 to 6
- values: bfloat16 [49152, 3072], P(('ctx', 'head')), may hold values from -6 to 6
- page_blocks: int32 [64, 2], replicated, may hold values from 1 to 5, as said below
- page_links: int32 [128, 16], replicated, may hold values from 0 to 127, as said below
- global_blocks: int32 [2], replicated, may hold values from 0 to 383
Outputs:
- attended: bfloat16 [49152, 3072], P(('ctx', 'head'))
Inputs may be any that keep to these rules, and one draw needn't show every extreme that they name: `page_links`: all 32 links of the pages of one ctx index name pages of distinct other ctx indices. `page_blocks`: each row sums to 6; some ctx index has a page of exactly 5 blocks.
All inputs are finite; a program needn't handle non-finite values.
Results may differ from a plain program's by a relative error of at most 0.0048.
Values may be sent and summed in bfloat16 or wider, within the bound.
A program may use at most 128 MiB of HBM per device.

v0:
```python
import jax
import jax.numpy as jnp
from jax import lax
from jax.sharding import PartitionSpec as P

HD = 128
BLK = 128
PAGES_DEV = 2
GROWS = 64
GB = 2
masked_score = -1e30


def shards(queries, keys, values, page_blocks, page_links, global_blocks):
    q_local, k_local, v_local = (
        lax.all_to_all(queries, "head", split_axis=1, concat_axis=0, tiled=True),
        lax.all_to_all(keys, "head", split_axis=1, concat_axis=0, tiled=True),
        lax.all_to_all(values, "head", split_axis=1, concat_axis=0, tiled=True),
    )
    ctx_count = lax.axis_size("ctx")
    my_index = lax.axis_index("ctx")
    rows = q_local.shape[0]
    width = q_local.shape[1]
    n_heads = width // HD
    n_blocks = rows // BLK
    link_count = page_links.shape[1]
    my_lengths = lax.dynamic_slice_in_dim(page_blocks, my_index, 1, 0)[0]
    my_starts = jnp.cumsum(my_lengths) - my_lengths
    block_ids = jnp.arange(n_blocks, dtype=jnp.int32)
    block_page = jnp.sum((block_ids[:, None] >= my_starts[None, :]).astype(jnp.int32), axis=1) - 1
    token_page = jnp.repeat(block_page, BLK)
    pair_kv = jnp.concatenate((k_local, v_local), axis=1)
    leaders = jnp.stack(
        [
            lax.dynamic_slice_in_dim(pair_kv, my_starts[page] * BLK, BLK, 0)
            for page in range(PAGES_DEV)
        ]
    )
    reader_links = page_links.reshape(ctx_count, PAGES_DEV * link_count)
    to_mine = reader_links // PAGES_DEV == my_index
    chosen = jnp.stack(
        [
            jnp.sum((to_mine & (reader_links % PAGES_DEV == page)).astype(jnp.float32), axis=1)
            for page in range(PAGES_DEV)
        ],
        axis=1,
    )
    chosen = jnp.minimum(chosen, 1.0).astype(jnp.bfloat16)
    outgoing = jnp.einsum(
        "rp,pbf->rbf", chosen, leaders, preferred_element_type=jnp.float32
    ).astype(jnp.bfloat16)
    incoming = lax.all_to_all(outgoing, "ctx", split_axis=0, concat_axis=0, tiled=True)
    my_links = lax.dynamic_slice_in_dim(page_links, my_index * PAGES_DEV, PAGES_DEV, 0)
    sources = my_links // PAGES_DEV
    span = GROWS // GB
    owners = global_blocks // n_blocks
    places = global_blocks % n_blocks
    pieces = [
        jnp.where(
            owners[i] == my_index,
            lax.dynamic_slice_in_dim(pair_kv, places[i] * BLK, span, 0).astype(jnp.float32),
            0.0,
        )
        for i in range(GB)
    ]
    global_kv = lax.psum(jnp.concatenate(pieces, 0), "ctx").astype(jnp.bfloat16)
    scale = HD ** (-0.5)
    k_own = k_local.reshape(rows, n_heads, HD)
    v_own = v_local.reshape(rows, n_heads, HD)
    g_keys = global_kv[:, :width].reshape(GROWS, n_heads, HD)
    g_values = global_kv[:, width:].reshape(GROWS, n_heads, HD)
    group_size = 1
    for count in range(1, n_blocks + 1):
        if n_blocks % count == 0 and count * BLK <= 512:
            group_size = count
    n_groups = n_blocks // group_size
    q_groups = q_local.reshape(n_groups, group_size, BLK, n_heads, HD)
    page_groups = block_page.reshape(n_groups, group_size)

    def attend_group(operands):
        q_blocks, group_page = operands
        s_own = (
            jnp.einsum("bqhd,khd->bhqk", q_blocks, k_own, preferred_element_type=jnp.float32)
            * scale
        )
        own_mask = group_page[:, None] == token_page[None, :]
        s_own = jnp.where(own_mask[:, None, None, :], s_own, masked_score)
        s_glob = (
            jnp.einsum("bqhd,ghd->bhqg", q_blocks, g_keys, preferred_element_type=jnp.float32)
            * scale
        )
        block_kv = incoming[sources[group_page]].reshape(group_size, link_count * BLK, 2 * width)
        l_keys = block_kv[:, :, :width].reshape(group_size, link_count * BLK, n_heads, HD)
        l_values = block_kv[:, :, width:].reshape(group_size, link_count * BLK, n_heads, HD)
        s_link = (
            jnp.einsum("bqhd,bkhd->bhqk", q_blocks, l_keys, preferred_element_type=jnp.float32)
            * scale
        )
        row_max = jnp.maximum(
            jnp.maximum(jnp.max(s_own, axis=3), jnp.max(s_glob, axis=3)), jnp.max(s_link, axis=3)
        )
        w_link = jnp.exp(s_link - row_max[..., None])
        total_link = jnp.sum(w_link, axis=3)
        mixed_link = jnp.einsum(
            "bhqk,bkhd->bqhd",
            w_link.astype(jnp.bfloat16),
            l_values,
            preferred_element_type=jnp.float32,
        )
        w_own = jnp.exp(s_own - row_max[..., None])
        w_glob = jnp.exp(s_glob - row_max[..., None])
        total = jnp.sum(w_own, axis=3) + jnp.sum(w_glob, axis=3) + total_link
        mixed = jnp.einsum(
            "bhqk,khd->bqhd", w_own.astype(jnp.bfloat16), v_own, preferred_element_type=jnp.float32
        )
        mixed = mixed + jnp.einsum(
            "bhqg,ghd->bqhd",
            w_glob.astype(jnp.bfloat16),
            g_values,
            preferred_element_type=jnp.float32,
        )
        mixed = mixed + mixed_link
        mixed = mixed / jnp.transpose(total, (0, 2, 1))[..., None]
        return mixed.astype(jnp.bfloat16)

    result = lax.map(attend_group, (q_groups, page_groups)).reshape(rows, width)
    return lax.all_to_all(result, "head", split_axis=0, concat_axis=1, tiled=True)


def solution(mesh):
    return jax.shard_map(
        shards,
        mesh=mesh,
        in_specs=(
            P(("ctx", "head"), None),
            P(("ctx", "head"), None),
            P(("ctx", "head"), None),
            P(),
            P(),
            P(),
        ),
        out_specs=P(("ctx", "head"), None),
        check_vma=False,
    )
```

profile of v0, /device:TPU:256, one launch (start us, length us, event | category | flops | bytes accessed | tf_op | source)
XLA Modules:
  0.0 931.5 jit_solution(17150689993805457864)
XLA Ops:
  0.0 2.0 copy.230
  2.0 4.3 all-to-all-start.1
  6.3 1.9 copy.229
  8.2 9.1 all-to-all-done.1
  17.4 3.5 all-to-all-start.2
  24.5 7.4 all-to-all-done.2
  31.9 3.5 all-to-all-start
  37.6 4.6 convolution_convert_fusion
  42.2 22.8 %copy.181 = bf16[64,128,768]{2,1,0:T(8,128)(2,1)} copy(bf16[64,128,768]{2,0,1:T(8,128)(2,1)S(1)} %convolution_convert_fusion) | data formatting | bytes 25165824 | tf_op jit(solution)/shard_map/convert_element_type | solution.py:51
  65.9 13.3 %all-to-all-start.3 = ((bf16[64,128,768]{2,1,0:T(8,128)(2,1)}), bf16[64,128,768]{2,1,0:T(8,128)(2,1)}, u32[]{:S(2)}, u32[]{:S(2)}) async-start(bf16[64,128,768]{2,1,0:T(8,128)(2,1)} %copy.181), calls=%async_computation.3 | async-start | bytes 25165824 | tf_op jit(solution)/shard_map/all_to_all | solution.py:52
  82.9 1.3 sub.53
  84.4 708.6 %all-reduce.1 = bf16[64,768]{1,0:T(8,128)(2,1)S(1)} all-reduce(f32[64,768]{1,0:T(8,128)S(1)} %pad_maximum_fusion), channel_id=1, replica_groups=mesh['ctx'=64,'head'=8] {'ctx'}, use_global_device_ids=true, to_apply=%region_2.3 | all-reduce | flops 49152 | bytes 294912 | tf_op jit(solution)/shard_map/psum | solution.py:66
  797.8 112.3 %while.11 = (s32[]{:T(128)}, bf16[2,3,128,3,128]{4,2,1,3,0:T(8,128)(2,1)}, s32[2,3]{1,0:T(2,128)}, bf16[2,3,128,3,128]{4,2,1,3,0:T(8,128)(2,1)}, bf16[768,3,128]...) while((s32[]{:T(128)}, ...), condition=%wide.region_14.15_spmd.clone, body=%wide.region_7.14_spmd.clone.sunk | while | flops 1723615360 | bytes 118326752 | solution.py:126
  799.2 2.5 bitcast_reduce_fusion.2
  804.2 10.7 %gather_fusion.1 = bf16[48,128,768]{2,1,0:T(8,128)(2,1)} fusion(bf16[64,128,768]{2,1,0:T(8,128)(2,1)} %get-tuple-element.344, s32[1024]{0:T(1024)S(1)} %pad_clamp_fusion.5), kind=kCustom, calls=%fused_computation.1.clone.clone.1 | custom fusion | bytes 18874560 | tf_op jit(solution)/shard_map/while/body/eval_jaxpr/gather | solution.py:92
  814.9 8.4 fusion.102
  823.2 6.7 copy.247
  830.0 4.0 multiply_reduce_fusion.2
  834.3 3.9 fusion.105
  839.8 6.7 copy.249
  846.5 5.2 fusion.106
  852.7 1.1 fusion.111
  855.3 2.5 bitcast_reduce_fusion.2
  860.2 10.9 %gather_fusion.1 = bf16[48,128,768]{2,1,0:T(8,128)(2,1)} fusion(bf16[64,128,768]{2,1,0:T(8,128)(2,1)} %get-tuple-element.344, s32[1024]{0:T(1024)S(1)} %pad_clamp_fusion.5), kind=kCustom, calls=%fused_computation.1.clone.clone.1 | custom fusion | bytes 18874560 | tf_op jit(solution)/shard_map/while/body/eval_jaxpr/gather | solution.py:92
  871.1 8.4 fusion.102
  879.5 6.7 copy.247
  886.2 4.0 multiply_reduce_fusion.2
  890.5 3.9 fusion.105
  896.0 6.7 copy.249
  902.7 5.2 fusion.106
  910.1 1.6 copy.188
  912.2 18.4 %all_to_all.78 = bf16[8,96,384]{2,1,0:T(8,128)(2,1)S(1)} all-to-all(bf16[8,96,384]{2,1,0:T(8,128)(2,1)S(1)} %all_to_all.69), channel_id=1, replica_groups=mesh['ctx'=64,'head'=8] {'head'}, dimensions={0} | all-to-all | bytes 1179648 | tf_op jit(solution)/shard_map/all_to_all | solution.py:127
  (117 shorter events, 27.7 us)
Async XLA Ops:
  0.0 20.9 %copy-start = (s32[64,2]{0,1:T(2,128)S(1)}, s32[64,2]{0,1:T(2,128)}, u32[]{:S(2)}) copy-start(s32[64,2]{0,1:T(2,128)} %param.11) | copy-start | bytes 1540
  0.0 23.1 %copy-start.13 = (s32[128,16]{0,1:T(8,128)S(1)}, s32[128,16]{0,1:T(8,128)}, u32[]{:S(2)}) copy-start(s32[128,16]{0,1:T(8,128)} %param.12) | copy-start | bytes 24580
  0.0 23.6 %copy-start.9 = (bf16[96,3072]{1,0:T(8,128)(2,1)S(1)}, bf16[96,3072]{1,0:T(8,128)(2,1)}, u32[]{:S(2)}) copy-start(bf16[96,3072]{1,0:T(8,128)(2,1)} %param.8) | copy-start | bytes 1769476
  2.0 15.4 %all-to-all-start.1 = ((bf16[96,8,384]{2,0,1:T(8,128)(2,1)}), bf16[96,8,384]{2,0,1:T(8,128)(2,1)S(1)}, u32[]{:S(2)}, u32[]{:S(2)}) async-start(bf16[96,8,384]{2,0,1:T(8,128)(2,1)} %bitcast.138), calls=%async_computation.1 | async-start | bytes 1179648 | tf_op jit(solution)/shard_map/all_to_all | solution.py:17
  17.4 14.5 %all-to-all-start.2 = ((bf16[96,8,384]{2,0,1:T(8,128)(2,1)}), bf16[96,8,384]{2,0,1:T(8,128)(2,1)S(1)}, u32[]{:S(2)}, u32[]{:S(2)}) async-start(bf16[96,8,384]{2,0,1:T(8,128)(2,1)} %bitcast.137), calls=%async_computation.2 | async-start | bytes 1179648 | tf_op jit(solution)/shard_map/all_to_all | solution.py:18
  31.9 33.1 %all-to-all-start = ((bf16[96,8,384]{2,0,1:T(8,128)(2,1)}), bf16[96,8,384]{2,0,1:T(8,128)(2,1)S(1)}, u32[]{:S(2)}, u32[]{:S(2)}) async-start(bf16[96,8,384]{2,0,1:T(8,128)(2,1)} %bitcast.139), calls=%async_computation | async-start | bytes 1179648 | tf_op jit(solution)/shard_map/all_to_all | solution.py:16
  65.0 14.2 %copy-start.14 = (s32[2]{0:T(128)S(1)}, s32[2]{0:T(128)}, u32[]{:S(2)}) copy-start(s32[2]{0:T(128)} %param.13) | copy-start | bytes 28
  65.0 0.9 copy-start.5
  65.9 731.9 %all-to-all-start.3 = ((bf16[64,128,768]{2,1,0:T(8,128)(2,1)}), bf16[64,128,768]{2,1,0:T(8,128)(2,1)}, u32[]{:S(2)}, u32[]{:S(2)}) async-start(bf16[64,128,768]{2,1,0:T(8,128)(2,1)} %copy.181), calls=%async_computation.3 | async-start | bytes 25165824 | tf_op jit(solution)/shard_map/all_to_all | solution.py:52
  79.2 717.3 %copy-start.6 = (bf16[96,8,384]{2,0,1:T(8,128)(2,1)S(1)}, bf16[96,8,384]{2,0,1:T(8,128)(2,1)}, u32[]{:S(2)}) copy-start(bf16[96,8,384]{2,0,1:T(8,128)(2,1)} %copy-done.5) | copy-start | bytes 1769476
  829.9 4.0 copy-start.2
  829.9 4.0 copy-start.7
  830.0 4.3 copy-start.8
  834.2 4.9 copy-start.3
  846.5 5.2 copy-start.10
  851.7 1.0 copy-start.4
  851.7 1.0 copy-start.11
  851.7 1.0 copy-start.12
  886.2 4.0 copy-start.2
  886.2 4.0 copy-start.7
  886.2 4.3 copy-start.8
  890.5 4.9 copy-start.3
  902.7 5.2 copy-start.10
  907.9 1.0 copy-start.4
  908.0 1.0 copy-start.11
  908.0 1.0 copy-start.12
  910.1 21.5 %copy-start.1 = (s32[64,2]{0,1:T(2,128)S(1)}, s32[64,2]{0,1:T(2,128)}, u32[]{:S(2)}) copy-start(s32[64,2]{0,1:T(2,128)} %param.11) | copy-start | bytes 1540
where the time goes:
time: 933 us; the launch traced here: 932 us
  blocking collectives  727 us (78%)
  local copies, waits for them, and re-layouts  112 us (12%)
  matrix products  32.5 us (3%)
  starting transfers between devices  24.7 us (3%)
  waiting for transfers between devices  16.5 us (2%)
  other arithmetic  15 us (2%)
    psum x1, blocking collectives, shards(): global_kv = lax.psum(jnp.concatenate(pieces, 0), 'ctx').astype(jnp.bfloat16)  709 us
    slice x4, local copies, waits for them, and re-layouts, attend_group(): block_kv[:, :, width:].reshape(group_size, link_count * BLK, n_heads, HD)  30.1 us
    convert_element_type x1, local copies, waits for them, and re-layouts, shards(): outgoing = jnp.einsum('rp,pbf->rbf', chosen, leaders, preferred_element_t...  22.8 us
    gather x2, local copies, waits for them, and re-layouts, attend_group(): incoming[sources[group_page]]  21.6 us
  transfers between devices with their start and end apart: 4, of which 2 were waited for; matrix products, arithmetic and copies ran while one was open for 4% of the time, Pallas kernels for 0%

commit v1 on v0

--- a/solution.py
+++ b/solution.py
@@ -9,6 +9,12 @@
 GROWS = 64
 GB = 2
 masked_score = -1e30
+
+
+def gather_and_add(shard, name):
+    parts = lax.all_gather(shard, name, axis=0, tiled=False)
+    acc = parts.sum(axis=0)
+    return acc
 
 
 def shards(queries, keys, values, page_blocks, page_links, global_blocks):
@@ -63,7 +69,7 @@
         )
         for i in range(GB)
     ]
-    global_kv = lax.psum(jnp.concatenate(pieces, 0), "ctx").astype(jnp.bfloat16)
+    global_kv = gather_and_add(jnp.concatenate(pieces, 0), "ctx").astype(jnp.bfloat16)
     scale = HD ** (-0.5)
     k_own = k_local.reshape(rows, n_heads, HD)
     v_own = v_local.reshape(rows, n_heads, HD)

time: 933 us -> 715 us (0.77)
  the two profiles are of different devices: /device:TPU:256 before, /device:TPU:152 now
where the time goes in v1:
time: 715 us; the launch traced here: 713 us
  waiting for transfers between devices  409 us (57%)
  local copies, waits for them, and re-layouts  111 us (16%)
  blocking collectives  95.5 us (13%)
  matrix products  32.5 us (5%)
  starting transfers between devices  26.1 us (4%)
  other arithmetic  20.8 us (3%)
  between operations  17.4 us (2%)
    all_gather x1, waiting for transfers between devices, gather_and_add(): parts = lax.all_gather(shard, name, axis=0, tiled=False)  372 us
    all_to_all x1, blocking collectives, shards(): lax.all_to_all(result, 'head', split_axis=0, concat_axis=1, tiled=True)  95.5 us
    slice x4, local copies, waits for them, and re-layouts, attend_group(): block_kv[:, :, width:].reshape(group_size, link_count * BLK, n_heads, HD)  30.2 us
    all_to_all x1, waiting for transfers between devices, shards(): lax.all_to_all(outgoing, 'ctx', split_axis=0, concat_axis=0, tiled=True)  23.5 us
    convert_element_type x1, local copies, waits for them, and re-layouts, shards(): outgoing = jnp.einsum('rp,pbf->rbf', chosen, leaders, preferred_element_t...  22.8 us
    gather x2, local copies, waits for them, and re-layouts, attend_group(): incoming[sources[group_page]]  21.6 us
    all_to_all x1, starting transfers between devices, shards(): lax.all_to_all(outgoing, 'ctx', split_axis=0, concat_axis=0, tiled=True)  14.7 us
  transfers between devices with their start and end apart: 5, of which 4 were waited for; matrix products, arithmetic and copies ran while one was open for 7% of the time, Pallas kernels for 0%

profile of v1, /device:TPU:152, one launch (start us, length us, event | category | flops | bytes accessed | tf_op | source)
XLA Modules:
  0.0 713.2 jit_solution(2316156941984708707)
XLA Ops:
  6.5 2.0 copy.230
  8.5 4.3 all-to-all-start.1
  13.2 1.9 copy.229
  15.1 8.8 %all-to-all-done.1 = bf16[96,8,384]{2,0,1:T(8,128)(2,1)S(1)} async-done(((bf16[96,8,384]{2,0,1:T(8,128)(2,1)}), bf16[96,8,384]{2,0,1:T(8,128)(2,1)S(1)}, u32[]{:S(2)}, u32[]{:S(2)}) %all-to-all-start.1) | async-done | bytes 589856 | tf_op jit(solution)/shard_map/all_to_all | solution.py:23
  23.9 3.5 all-to-all-start.2
  33.9 4.5 all-to-all-done.2
  38.4 3.5 all-to-all-start
  44.9 4.6 convolution_convert_fusion
  49.5 22.8 %copy.181 = bf16[64,128,768]{2,1,0:T(8,128)(2,1)} copy(bf16[64,128,768]{2,0,1:T(8,128)(2,1)S(1)} %convolution_convert_fusion) | data formatting | bytes 25165824 | tf_op jit(solution)/shard_map/convert_element_type | solution.py:57
  73.1 14.7 %all-to-all-start.3 = ((bf16[64,128,768]{2,1,0:T(8,128)(2,1)}), bf16[64,128,768]{2,1,0:T(8,128)(2,1)}, u32[]{:S(2)}, u32[]{:S(2)}) async-start(bf16[64,128,768]{2,1,0:T(8,128)(2,1)} %copy.181), calls=%async_computation.3 | async-start | bytes 25165824 | tf_op jit(solution)/shard_map/all_to_all | solution.py:58
  93.3 372.4 %all-gather.3.cloned.1.call-done = f32[4096,768]{1,0:T(8,128)} async-done(((f32[64,768]{1,0:T(8,128)}), f32[4096,768]{1,0:T(8,128)}) %all-gather.3.cloned.1.call-update) | async-done | bytes 12582928 | tf_op jit(solution)/shard_map/all_gather | solution.py:15
  465.7 5.2 reduce_sum.78
  472.1 23.5 %all-to-all-done.3 = bf16[64,128,768]{2,1,0:T(8,128)(2,1)} async-done(((bf16[64,128,768]{2,1,0:T(8,128)(2,1)}), bf16[64,128,768]{2,1,0:T(8,128)(2,1)}, u32[]{:S(2)}, u32[]{:S(2)}) %all-to-all-start.3) | async-done | bytes 12582944 | tf_op jit(solution)/shard_map/all_to_all | solution.py:58
  495.6 112.2 %while.11 = (s32[]{:T(128)}, bf16[2,3,128,3,128]{4,2,1,3,0:T(8,128)(2,1)}, s32[2,3]{1,0:T(2,128)}, bf16[2,3,128,3,128]{4,2,1,3,0:T(8,128)(2,1)}, bf16[768,3,128]...) while((s32[]{:T(128)}, ...), condition=%wide.region_14.15_spmd.clone, body=%wide.region_7.14_spmd.clone.sunk | while | flops 1723615360 | bytes 118326752 | solution.py:132
  497.0 2.5 bitcast_reduce_fusion.2
  502.0 10.7 %gather_fusion.1 = bf16[48,128,768]{2,1,0:T(8,128)(2,1)} fusion(bf16[64,128,768]{2,1,0:T(8,128)(2,1)} %get-tuple-element.344, s32[1024]{0:T(1024)S(1)} %pad_clamp_fusion.5), kind=kCustom, calls=%fused_computation.1.clone.clone.1 | custom fusion | bytes 18874560 | tf_op jit(solution)/shard_map/while/body/eval_jaxpr/gather | solution.py:98
  512.6 8.4 %fusion.102 = (bf16[3,2048,384]{2,1,0:T(8,128)(2,1)}, bf16[3,2048,384]{2,1,0:T(8,128)(2,1)}) fusion(bf16[3,2048,768]{2,1,0:T(8,128)(2,1)} %bitcast.193), kind=kLoop, calls=%fused_computation.116.clone.1 | loop fusion | bytes 18874368 | tf_op jit(solution)/shard_map/while/body/eval_jaxpr/slice | solution.py:100
  521.0 6.7 copy.247
  527.7 4.0 multiply_reduce_fusion.2
  532.0 3.9 fusion.105
  537.5 6.7 copy.249
  544.2 5.2 fusion.106
  553.0 2.5 bitcast_reduce_fusion.2
  557.9 10.9 %gather_fusion.1 = bf16[48,128,768]{2,1,0:T(8,128)(2,1)} fusion(bf16[64,128,768]{2,1,0:T(8,128)(2,1)} %get-tuple-element.344, s32[1024]{0:T(1024)S(1)} %pad_clamp_fusion.5), kind=kCustom, calls=%fused_computation.1.clone.clone.1 | custom fusion | bytes 18874560 | tf_op jit(solution)/shard_map/while/body/eval_jaxpr/gather | solution.py:98
  568.9 8.4 %fusion.102 = (bf16[3,2048,384]{2,1,0:T(8,128)(2,1)}, bf16[3,2048,384]{2,1,0:T(8,128)(2,1)}) fusion(bf16[3,2048,768]{2,1,0:T(8,128)(2,1)} %bitcast.193), kind=kLoop, calls=%fused_computation.116.clone.1 | loop fusion | bytes 18874368 | tf_op jit(solution)/shard_map/while/body/eval_jaxpr/slice | solution.py:100
  577.2 6.7 copy.247
  583.9 4.0 multiply_reduce_fusion.2
  588.2 3.9 fusion.105
  593.7 6.7 copy.249
  600.5 5.2 fusion.106
  607.8 1.6 copy.188
  609.9 95.5 %all_to_all.78 = bf16[8,96,384]{2,1,0:T(8,128)(2,1)S(1)} all-to-all(bf16[8,96,384]{2,1,0:T(8,128)(2,1)S(1)} %all_to_all.69), channel_id=1, replica_groups=mesh['ctx'=64,'head'=8] {'head'}, dimensions={0} | all-to-all | bytes 1179648 | tf_op jit(solution)/shard_map/all_to_all | solution.py:133
  (120 shorter events, 30.6 us)
Async XLA Ops:
  6.5 6.3 copy-start
  6.5 22.7 %copy-start.14 = (s32[2]{0:T(128)S(1)}, s32[2]{0:T(128)}, u32[]{:S(2)}) copy-start(s32[2]{0:T(128)} %param.13) | copy-start | bytes 28
  6.5 24.6 %copy-start.13 = (s32[128,16]{0,1:T(8,128)S(1)}, s32[128,16]{0,1:T(8,128)}, u32[]{:S(2)}) copy-start(s32[128,16]{0,1:T(8,128)} %param.12) | copy-start | bytes 24580
  6.5 26.5 %copy-start.9 = (bf16[96,3072]{1,0:T(8,128)(2,1)S(1)}, bf16[96,3072]{1,0:T(8,128)(2,1)}, u32[]{:S(2)}) copy-start(bf16[96,3072]{1,0:T(8,128)(2,1)} %param.8) | copy-start | bytes 1769476
  8.5 15.4 %all-to-all-start.1 = ((bf16[96,8,384]{2,0,1:T(8,128)(2,1)}), bf16[96,8,384]{2,0,1:T(8,128)(2,1)S(1)}, u32[]{:S(2)}, u32[]{:S(2)}) async-start(bf16[96,8,384]{2,0,1:T(8,128)(2,1)} %bitcast.139), calls=%async_computation.1 | async-start | bytes 1179648 | tf_op jit(solution)/shard_map/all_to_all | solution.py:23
  23.9 14.5 %all-to-all-start.2 = ((bf16[96,8,384]{2,0,1:T(8,128)(2,1)}), bf16[96,8,384]{2,0,1:T(8,128)(2,1)S(1)}, u32[]{:S(2)}, u32[]{:S(2)}) async-start(bf16[96,8,384]{2,0,1:T(8,128)(2,1)} %bitcast.138), calls=%async_computation.2 | async-start | bytes 1179648 | tf_op jit(solution)/shard_map/all_to_all | solution.py:24
  38.4 33.9 %all-to-all-start = ((bf16[96,8,384]{2,0,1:T(8,128)(2,1)}), bf16[96,8,384]{2,0,1:T(8,128)(2,1)S(1)}, u32[]{:S(2)}, u32[]{:S(2)}) async-start(bf16[96,8,384]{2,0,1:T(8,128)(2,1)} %bitcast.140), calls=%async_computation | async-start | bytes 1179648 | tf_op jit(solution)/shard_map/all_to_all | solution.py:22
  42.0 423.7 %all-gather.3.cloned.1.call-start = ((), (), s32[]{:S(2)}) async-start(), calls=%async_computation.5 | async-start | bytes 12779520 | tf_op jit(solution)/shard_map/all_gather | solution.py:15
  72.3 0.8 copy-start.5
  73.1 422.5 %all-to-all-start.3 = ((bf16[64,128,768]{2,1,0:T(8,128)(2,1)}), bf16[64,128,768]{2,1,0:T(8,128)(2,1)}, u32[]{:S(2)}, u32[]{:S(2)}) async-start(bf16[64,128,768]{2,1,0:T(8,128)(2,1)} %copy.181), calls=%async_computation.3 | async-start | bytes 25165824 | tf_op jit(solution)/shard_map/all_to_all | solution.py:58
  87.8 4.3 copy-start.6
  527.7 4.0 copy-start.2
  527.7 4.0 copy-start.7
  527.7 4.3 copy-start.8
  531.9 4.9 copy-start.3
  544.2 5.2 copy-start.10
  549.4 1.0 copy-start.4
  549.5 1.0 copy-start.11
  549.5 1.0 copy-start.12
  583.9 4.0 copy-start.2
  583.9 4.0 copy-start.7
  583.9 4.3 copy-start.8
  588.2 4.9 copy-start.3
  600.5 5.2 copy-start.10
  605.7 1.0 copy-start.4
  605.7 1.0 copy-start.11
  605.7 1.0 copy-start.12
  607.8 98.5 %copy-start.1 = (s32[64,2]{0,1:T(2,128)S(1)}, s32[64,2]{0,1:T(2,128)}, u32[]{:S(2)}) copy-start(s32[64,2]{0,1:T(2,128)} %param.11) | copy-start | bytes 1540
Sparse Core Ops, SparseCore 0:
  45.8 419.8 all-gather.2
